TPU v7x, 512 devices: a whole 4x8x8 slice. The times are simulated.
512 devices in a mesh: node: 64 (over y_lo, z, core), win: 8 (over y_hi, x).
Axes of the slice: x: 4, y: 8 (y_hi: 2, y_lo: 4; y = y_hi * 4 + y_lo), z: 8, core: 2. Of those that a mesh axis runs over, the one named last changes fastest.
Arguments:
- features: bfloat16 [32768, 8, 2, 128], P('node', 'win'), may hold values from -6 to 6
- node_vectors: float32 [32768, 128], P('node'), may hold values from -0.3 to 0.3
- projections: float32 [2, 64, 64], replicated, may hold values from -0.75 to 0.75
- mix_weight: bfloat16 [3, 128, 128], replicated, may hold values from -0.3125 to 0.3125
- region_sizes: int32 [128], replicated, may hold values from 1 to 4, 256 in all
- cotangent: bfloat16 [32768, 8, 2, 128], P('node', 'win'), may hold values from -6 to 6
Outputs:
- layer_output: bfloat16 [32768, 8, 2, 128], P('node', 'win')
- vector_grad: float32 [32768, 128], P('node')
- weight_grad: float32 [3, 128, 128], replicated
Inputs may be any that keep to these rules, and one draw needn't show every extreme that they name: `region_sizes`: each entry is a region size in units of 128 nodes; the entries sum to 256, and the largest region has 512 nodes.
All inputs are finite; a program needn't handle non-finite values.
Results may differ from a plain program's by a relative error of at most 0.015.
Values may be sent and summed in bfloat16 or wider, within the bound.
No kernel may reach another device: no remote copies, remote signals or barrier semaphores. Data moves between devices by JAX's collectives and lax.ppermute only.
A program may use at most 64 MiB of HBM per device.

v0:
```python
from functools import partial
import math
import jax
import jax.numpy as jnp
from jax import lax
from jax.sharding import PartitionSpec as P

BLOCK = 128
KEEP_INPUT = 0.05
ROWS_DIMS = (((1,), (1,)), ((), ()))
COLS_DIMS = (((0,), (0,)), ((), ()))


def padded(cells, sides, width):
    for axis, dim in sides:
        count = lax.axis_size(axis)
        ends = count - 1
        head = lax.slice_in_dim(cells, 0, width, axis=dim)
        tail = lax.slice_in_dim(cells, cells.shape[dim] - width, cells.shape[dim], axis=dim)
        cells = jnp.concatenate(
            [
                lax.ppermute(tail, axis, [(i, (i + 1) % count) for i in range(ends)]),
                cells,
                lax.ppermute(head, axis, [((i + 1) % count, i) for i in range(ends)]),
            ],
            axis=dim,
        )
    return cells


def shifted(block, axis, distance):
    devices = range(lax.axis_size(axis))
    route = [(i - distance, i) for i in devices if i - distance in devices]
    return lax.ppermute(block, axis, route)


def swapped(vectors):
    emb_half = vectors.shape[1] // 2
    return jnp.concatenate([vectors[:, emb_half:], -vectors[:, :emb_half]], axis=1)


def node_regions(region_sizes, node_index, node_total):
    region_ends = jnp.cumsum(region_sizes) * BLOCK
    region_index = jnp.sum((region_ends[None, :] <= node_index[:, None]).astype(jnp.int32), axis=1)
    in_range = (node_index >= 0) & (node_index < node_total)
    return jnp.where(in_range, region_index, -1)


def node_rim(values):
    return padded(values, (("node", 0),), values.shape[0])


def node_pass(values, offset_by):
    return shifted(values.astype(jnp.bfloat16), "node", offset_by).astype(values.dtype)


def spread_back(parts, node_count):
    lower = parts[:node_count]
    middle = parts[node_count : 2 * node_count]
    upper = parts[2 * node_count :]
    return middle + node_pass(lower, -1) + node_pass(upper, 1)


def dense_product(adj_rounded, wide_rows):
    return jnp.dot(adj_rounded, wide_rows, preferred_element_type=jnp.float32)


def body(features, node_vectors, projections, mix_weight, region_sizes, cotangent):
    node_count = features.shape[0]
    windows_dev = features.shape[1]
    steps_dev = features.shape[2]
    channels = features.shape[3]
    row_width = windows_dev * steps_dev * channels
    emb_half = node_vectors.shape[1] // 2
    node_total = node_count * lax.axis_size("node")
    first_node = lax.axis_index("node") * node_count
    own_index = first_node + jnp.arange(node_count, dtype=jnp.int32)
    wide_index = first_node - node_count + jnp.arange(3 * node_count, dtype=jnp.int32)
    own_region = node_regions(region_sizes, own_index, node_total)
    wide_region = node_regions(region_sizes, wide_index, node_total)
    highest = lax.Precision.HIGHEST
    source_m = jnp.tanh(
        3.0
        * jnp.dot(
            node_vectors[:, :emb_half],
            projections[0],
            precision=highest,
            preferred_element_type=jnp.float32,
        )
    )
    target_m = jnp.tanh(
        3.0
        * jnp.dot(
            node_vectors[:, emb_half:],
            projections[1],
            precision=highest,
            preferred_element_type=jnp.float32,
        )
    )
    learned = jnp.concatenate([source_m, target_m], axis=1).astype(jnp.bfloat16)
    inputs = features.reshape(node_count, row_width)
    rim_block = node_rim(jnp.concatenate([inputs, learned], axis=1))
    wide_inputs = rim_block[:, :row_width]
    wide_learned = rim_block[:, row_width:]
    scores = lax.dot_general(
        learned, swapped(wide_learned), ROWS_DIMS, preferred_element_type=jnp.float32
    )
    same_region = (own_region[:, None] == wide_region[None, :]) & (wide_region[None, :] >= 0)
    squashed = jnp.tanh(3.0 * scores)
    positive = jnp.maximum(squashed, 0.0)
    adjacency = jnp.where(same_region, positive * positive, 0.0)
    degree = 1.0 + jnp.sum(adjacency, axis=1)
    identity = (own_index[:, None] == wide_index[None, :]).astype(jnp.float32)
    adj_rounded = (adjacency + identity).astype(jnp.bfloat16)
    propagate = partial(dense_product, adj_rounded)
    inputs_f = inputs.astype(jnp.float32)
    prop_one = propagate(wide_inputs) / degree[:, None]
    hop_one = (KEEP_INPUT * inputs_f + (1.0 - KEEP_INPUT) * prop_one).astype(jnp.bfloat16)
    wide_one = node_rim(hop_one)
    prop_two = propagate(wide_one) / degree[:, None]
    hop_two = (KEEP_INPUT * inputs_f + (1.0 - KEEP_INPUT) * prop_two).astype(jnp.bfloat16)
    row_count = node_count * windows_dev * steps_dev
    hop_list = (inputs, hop_one, hop_two)
    mixed = jnp.zeros((row_count, channels), jnp.float32)
    for hop_order in range(3):
        mixed = mixed + jnp.dot(
            hop_list[hop_order].reshape(row_count, channels),
            mix_weight[hop_order],
            preferred_element_type=jnp.float32,
        )
    layer_output = mixed.astype(jnp.bfloat16).reshape(features.shape)
    upstream = cotangent.reshape(row_count, channels)
    norm_scale = 1.0 / math.sqrt(row_count * lax.axis_size("node") * lax.axis_size("win"))
    partial_mix = (
        jnp.stack(
            [
                lax.dot_general(
                    layer_rows.reshape(row_count, channels),
                    upstream,
                    COLS_DIMS,
                    preferred_element_type=jnp.float32,
                )
                for layer_rows in hop_list
            ]
        )
        * norm_scale
    )
    weight_grad = lax.psum(partial_mix, ("node", "win"))
    back_two = lax.dot_general(
        upstream, mix_weight[2], ROWS_DIMS, preferred_element_type=jnp.float32
    ).reshape(node_count, row_width)
    grad_two = ((1.0 - KEEP_INPUT) * back_two / degree[:, None]).astype(jnp.bfloat16)
    partials = lax.dot_general(adj_rounded, grad_two, COLS_DIMS, preferred_element_type=jnp.float32)
    carried = spread_back(partials, node_count)
    back_one = (
        lax.dot_general(
            upstream, mix_weight[1], ROWS_DIMS, preferred_element_type=jnp.float32
        ).reshape(node_count, row_width)
        + carried
    )
    grad_one = ((1.0 - KEEP_INPUT) * back_one / degree[:, None]).astype(jnp.bfloat16)
    pair_inner = lax.dot_general(
        jnp.concatenate([grad_one, grad_two], axis=1),
        jnp.concatenate([wide_inputs, wide_one], axis=1),
        ROWS_DIMS,
        preferred_element_type=jnp.float32,
    )
    offset = jnp.sum(grad_one.astype(jnp.float32) * prop_one, axis=1) + jnp.sum(
        grad_two.astype(jnp.float32) * prop_two, axis=1
    )
    score_grad = jnp.where(
        same_region,
        6.0 * (pair_inner - offset[:, None]) * positive * (1.0 - squashed * squashed),
        0.0,
    ).astype(jnp.bfloat16)
    row_part = jnp.dot(score_grad, swapped(wide_learned), preferred_element_type=jnp.float32)
    column_part = -lax.dot_general(
        score_grad, swapped(learned), COLS_DIMS, preferred_element_type=jnp.float32
    )
    grad_m = row_part + spread_back(column_part, node_count)
    source_grad = jnp.dot(
        3.0 * (1.0 - source_m * source_m) * grad_m[:, :emb_half],
        projections[0].T,
        precision=highest,
        preferred_element_type=jnp.float32,
    )
    target_grad = jnp.dot(
        3.0 * (1.0 - target_m * target_m) * grad_m[:, emb_half:],
        projections[1].T,
        precision=highest,
        preferred_element_type=jnp.float32,
    )
    vector_grad = lax.psum(
        jnp.concatenate([source_grad, target_grad], axis=1).astype(jnp.bfloat16), "win"
    ).astype(jnp.float32)
    return (layer_output, vector_grad, weight_grad)


def solution(mesh):
    placed = (
        P("node", "win", None, None),
        P("node", None),
        P(),
        P(),
        P(),
        P("node", "win", None, None),
    )
    return jax.shard_map(
        body,
        mesh=mesh,
        in_specs=placed,
        out_specs=(P("node", "win", None, None), P("node", None), P()),
        check_vma=False,
    )
```

profile of v0, /device:TPU:1, one launch (start us, length us, event | category | flops | bytes accessed | tf_op | source)
XLA Modules:
  0.0 480.1 jit_solution(4617464330748801811)
XLA Ops:
  7.2 2.1 fusion.88
  9.4 2.1 fusion.83
  11.6 1.0 copy.51
  12.8 8.8 %collective-permute-start.1 = (bf16[512,384]{1,0:T(8,128)(2,1)S(1)}, bf16[512,384]{1,0:T(8,128)(2,1)S(1)}, u32[]{:S(2)}, u32[]{:S(2)}) collective-permute-start(bf16[512,384]{1,0:T(8,128)(2,1)S(1)} %pad_maximum_fusion.1), channel_id=1, source_target_pairs={{8,0},{16,8},{24,16},{32,24},{40,32},{48,40},{56,48},{64,56},{72,6... | collective-permute-start | bytes 1179656 | tf_op jit(solution)/shard_map/ppermute | solution.py:24
  21.6 1.9 collective-permute-start
  25.7 2.5 collective-permute-done
  28.6 3.3 fusion.6
  32.0 1.5 add_convert_fusion.2
  33.5 1.9 collective-permute-start.3
  35.4 4.4 collective-permute-start.2
  40.2 1.0 fusion.62
  41.2 1.0 collective-permute-done.3
  42.3 1.2 collective-permute-done.2
  43.4 3.5 multiply_reduce_fusion
  48.4 1.9 collective-permute-start.4
  50.3 4.4 collective-permute-start.5
  56.6 1.1 reshape.106
  57.7 2.2 convolution_add_fusion.1
  59.9 1.6 multiply_reduce_fusion.1
  61.6 2.9 fusion.5
  64.6 1.3 fusion.90
  66.6 2.0 collective-permute-start.6
  68.6 3.6 collective-permute-start.7
  73.3 1.2 collective-permute-done.7
  75.2 2.0 fusion.31
  77.2 1.1 convolution_convert_fusion
  78.2 1.0 convolution_convert_fusion.1
  81.1 1.7 fusion.14
  82.7 113.3 %all-reduce.3.cloned.1.call-done = bf16[512,128]{0,1:T(8,128)(2,1)} async-done(((bf16[512,128]{0,1:T(8,128)(2,1)}), bf16[512,128]{0,1:T(8,128)(2,1)}) %all-reduce.3.cloned.1.call-update) | async-done | bytes 131088 | tf_op jit(solution)/shard_map/psum | solution.py:193
  196.0 1.7 copy.38
  197.8 273.9 %all-reduce.5.cloned.1.call-done = f32[3,128,128]{2,1,0:T(8,128)} async-done(((f32[3,128,128]{2,1,0:T(8,128)}), f32[3,128,128]{2,1,0:T(8,128)}) %all-reduce.5.cloned.1.call-update) | async-done | bytes 196624 | tf_op jit(solution)/shard_map/psum | solution.py:148
  471.7 1.6 copy.54
  (95 shorter events, 10.7 us)
Async XLA Ops:
  7.2 17.5 %copy-start = (bf16[512,1,2,128]{3,2,1,0:T(2,128)(2,1)S(1)}, bf16[512,1,2,128]{3,2,1,0:T(2,128)(2,1)}, u32[]{:S(2)}) copy-start(bf16[512,1,2,128]{3,2,1,0:T(2,128)(2,1)} %param.11) | copy-start | bytes 786436
  7.2 16.4 %copy-start.26 = (s32[128]{0:T(128)S(1)}, s32[128]{0:T(128)}, u32[]{:S(2)}) copy-start(s32[128]{0:T(128)} %param.10) | copy-start | bytes 1540
  7.2 188.9 %all-reduce.3.cloned.1.call-start = ((), (), s32[]{:S(2)}) async-start(), calls=%async_computation | async-start | bytes 262144 | tf_op jit(solution)/shard_map/psum | solution.py:193
  9.4 19.2 %copy-start.10 = (bf16[512,64]{0,1:T(8,128)(2,1)}, bf16[512,64]{0,1:T(8,128)(2,1)S(1)}, u32[]{:S(2)}) copy-start(bf16[512,64]{0,1:T(8,128)(2,1)S(1)} %get-tuple-element.29) | copy-start | bytes 196612
  12.8 12.9 %collective-permute-start.1 = (bf16[512,384]{1,0:T(8,128)(2,1)S(1)}, bf16[512,384]{1,0:T(8,128)(2,1)S(1)}, u32[]{:S(2)}, u32[]{:S(2)}) collective-permute-start(bf16[512,384]{1,0:T(8,128)(2,1)S(1)} %pad_maximum_fusion.1), channel_id=1, source_target_pairs={{8,0},{16,8},{24,16},{32,24},{40,32},{48,40},{56,48},{64,56},{72,6... | collective-permute-start | bytes 1179656 | tf_op jit(solution)/shard_map/ppermute | solution.py:24
  21.6 6.6 %collective-permute-start = (bf16[512,384]{1,0:T(8,128)(2,1)S(1)}, bf16[512,384]{1,0:T(8,128)(2,1)S(1)}, u32[]{:S(2)}, u32[]{:S(2)}) collective-permute-start(bf16[512,384]{1,0:T(8,128)(2,1)S(1)} %pad_maximum_fusion.1), channel_id=1, source_target_pairs={{0,8},{8,16},{16,24},{24,32},{32,40},{40,48},{48,56},{56,64},{64,7... | collective-permute-start | bytes 1179656 | tf_op jit(solution)/shard_map/ppermute | solution.py:22
  24.7 3.9 copy-start.24
  28.4 28.2 %copy-start.1 = (bf16[1536,384]{1,0:T(8,128)(2,1)}, bf16[1536,384]{1,0:T(8,128)(2,1)S(1)}, u32[]{:S(2)}) copy-start(bf16[1536,384]{1,0:T(8,128)(2,1)S(1)} %pad_maximum_fusion) | copy-start | bytes 3538948
  28.6 3.4 copy-start.3
  28.6 3.4 copy-start.5
  32.0 7.8 %copy-start.14 = (bf16[3,128,128]{2,1,0:T(8,128)(2,1)S(1)}, bf16[3,128,128]{2,1,0:T(8,128)(2,1)}, u32[]{:S(2)}) copy-start(bf16[3,128,128]{2,1,0:T(8,128)(2,1)} %param.9) | copy-start | bytes 294916
  33.5 8.7 %collective-permute-start.3 = (bf16[512,256]{1,0:T(8,128)(2,1)}, bf16[512,256]{1,0:T(8,128)(2,1)}, u32[]{:S(2)}, u32[]{:S(2)}) collective-permute-start(bf16[512,256]{1,0:T(8,128)(2,1)} %get-tuple-element.33), channel_id=1, source_target_pairs={{8,0},{16,8},{24,16},{32,24},{40,32},{48,40},{56,48},{64,56},{72,6... | collective-permute-start | bytes 786440 | tf_op jit(solution)/shard_map/ppermute | solution.py:24
  35.4 8.0 %collective-permute-start.2 = (bf16[512,256]{1,0:T(8,128)(2,1)}, bf16[512,256]{1,0:T(8,128)(2,1)}, u32[]{:S(2)}, u32[]{:S(2)}) collective-permute-start(bf16[512,256]{1,0:T(8,128)(2,1)} %get-tuple-element.33), channel_id=1, source_target_pairs={{0,8},{8,16},{16,24},{24,32},{32,40},{40,48},{48,56},{56,64},{64,7... | collective-permute-start | bytes 786440 | tf_op jit(solution)/shard_map/ppermute | solution.py:22
  41.2 5.7 %copy-start.7 = (bf16[512,1536]{1,0:T(8,128)(2,1)S(1)}, bf16[512,1536]{1,0:T(8,128)(2,1)}, u32[]{:S(2)}) copy-start(bf16[512,1536]{1,0:T(8,128)(2,1)} %copy-done.6) | copy-start | bytes 4718596
  46.9 7.8 %copy-start.9 = (bf16[512,1,2,128]{3,2,1,0:T(2,128)(2,1)S(1)}, bf16[512,1,2,128]{3,2,1,0:T(2,128)(2,1)}, u32[]{:S(2)}) copy-start(bf16[512,1,2,128]{3,2,1,0:T(2,128)(2,1)} %param.6) | copy-start | bytes 786436
  48.4 11.6 %collective-permute-start.4 = (bf16[512,256]{1,0:T(8,128)(2,1)}, bf16[512,256]{1,0:T(8,128)(2,1)}, u32[]{:S(2)}, u32[]{:S(2)}) collective-permute-start(bf16[512,256]{1,0:T(8,128)(2,1)} %get-tuple-element.24), channel_id=1, source_target_pairs={{8,0},{16,8},{24,16},{32,24},{40,32},{48,40},{56,48},{64,56},{72,6... | collective-permute-start | bytes 786440 | tf_op jit(solution)/shard_map/ppermute | solution.py:34
  50.3 9.6 %collective-permute-start.5 = (bf16[512,256]{1,0:T(8,128)(2,1)}, bf16[512,256]{1,0:T(8,128)(2,1)}, u32[]{:S(2)}, u32[]{:S(2)}) collective-permute-start(bf16[512,256]{1,0:T(8,128)(2,1)} %get-tuple-element.25), channel_id=1, source_target_pairs={{0,8},{8,16},{16,24},{24,32},{32,40},{40,48},{48,56},{56,64},{64,7... | collective-permute-start | bytes 786440 | tf_op jit(solution)/shard_map/ppermute | solution.py:34
  56.5 5.0 %copy-start.23 = (f32[512]{0:T(512)S(1)}, f32[512]{0:T(512)}, u32[]{:S(2)}) copy-start(f32[512]{0:T(512)} %get-tuple-element.14) | copy-start | bytes 6148
  56.5 5.0 %slice-start = ((bf16[1536,384]{1,0:T(8,128)(2,1)}), bf16[1536,256]{1,0:T(8,128)(2,1)S(1)}, s32[]{:S(2)}) async-start(bf16[1536,384]{1,0:T(8,128)(2,1)} %copy-done.1), calls=%async_computation.2 | async-start | bytes 1572864 | tf_op jit(solution)/shard_map/slice | solution.py:103
  56.5 5.0 %copy-start.16 = (bf16[512,256]{1,0:T(8,128)(2,1)S(1)}, bf16[512,256]{1,0:T(8,128)(2,1)}, u32[]{:S(2)}) copy-start(bf16[512,256]{1,0:T(8,128)(2,1)} %copy-done.15) | copy-start | bytes 786436
  57.7 3.9 copy-start.25
  57.7 3.9 copy-start.27
  64.5 8.6 %copy-start.18 = (bf16[512,256]{1,0:T(8,128)(2,1)S(1)}, bf16[512,256]{1,0:T(8,128)(2,1)}, u32[]{:S(2)}) copy-start(bf16[512,256]{1,0:T(8,128)(2,1)} %get-tuple-element.26) | copy-start | bytes 786436
  64.5 10.6 %copy-start.4 = (bf16[1536,64]{1,0:T(8,128)(2,1)S(1)}, bf16[1536,64]{1,0:T(8,128)(2,1)}, u32[]{:S(2)}) copy-start(bf16[1536,64]{1,0:T(8,128)(2,1)} %copy-done.3) | copy-start | bytes 589828
  65.8 11.3 %copy-start.13 = (f32[512,64]{0,1:T(8,128)S(1)}, f32[512,64]{0,1:T(8,128)}, u32[]{:S(2)}) copy-start(f32[512,64]{0,1:T(8,128)} %get-tuple-element.30) | copy-start | bytes 393220
  66.6 11.7 %copy-start.12 = (f32[512,64]{0,1:T(8,128)S(1)}, f32[512,64]{0,1:T(8,128)}, u32[]{:S(2)}) copy-start(f32[512,64]{0,1:T(8,128)} %get-tuple-element.31) | copy-start | bytes 393220
  66.6 6.7 %collective-permute-start.6 = (bf16[512,128]{0,1:T(8,128)(2,1)}, bf16[512,128]{0,1:T(8,128)(2,1)S(1)}, u32[]{:S(2)}, u32[]{:S(2)}) collective-permute-start(bf16[512,128]{0,1:T(8,128)(2,1)} %get-tuple-element.27), channel_id=1, source_target_pairs={{8,0},{16,8},{24,16},{32,24},{40,32},{48,40},{56,48},{64,56},{72,6... | collective-permute-start | bytes 393224 | tf_op jit(solution)/shard_map/ppermute | solution.py:34
  68.6 5.9 %collective-permute-start.7 = (bf16[512,128]{0,1:T(8,128)(2,1)}, bf16[512,128]{0,1:T(8,128)(2,1)S(1)}, u32[]{:S(2)}, u32[]{:S(2)}) collective-permute-start(bf16[512,128]{0,1:T(8,128)(2,1)} %get-tuple-element.28), channel_id=1, source_target_pairs={{0,8},{8,16},{16,24},{24,32},{32,40},{40,48},{48,56},{56,64},{64,7... | collective-permute-start | bytes 393224 | tf_op jit(solution)/shard_map/ppermute | solution.py:34
  75.2 5.1 %copy-start.19 = (f32[1,128,128]{2,1,0:T(8,128)S(1)}, f32[1,128,128]{2,1,0:T(8,128)}, u32[]{:S(2)}) copy-start(f32[1,128,128]{2,1,0:T(8,128)} %convolution_bitcast_fusion.1) | copy-start | bytes 196612
  75.2 5.2 %copy-start.22 = (f32[1,128,128]{2,1,0:T(8,128)S(1)}, f32[1,128,128]{2,1,0:T(8,128)}, u32[]{:S(2)}) copy-start(f32[1,128,128]{2,1,0:T(8,128)} %convolution_bitcast_fusion.2) | copy-start | bytes 196612
  75.2 5.9 %copy-start.2 = (f32[1024,128]{1,0:T(8,128)S(1)}, f32[1024,128]{1,0:T(8,128)}, u32[]{:S(2)}) copy-start(f32[1024,128]{1,0:T(8,128)} %convolution_add_fusion.1) | copy-start | bytes 1572868
  80.0 391.7 %all-reduce.5.cloned.1.call-start = ((), (), s32[]{:S(2)}) async-start(), calls=%async_computation.1 | async-start | bytes 393216 | tf_op jit(solution)/shard_map/psum | solution.py:148
  (7 other events, 14.2 us)
Sparse Core Ops, SparseCore 0:
  80.1 115.9 all-reduce.2
  201.6 270.0 all-reduce.4
where the time goes:
time: 481 us; the launch traced here: 480 us
  waiting for transfers between devices  393 us (82%)
  matrix products  29.5 us (6%)
  starting transfers between devices  29 us (6%)
  between operations  14.6 us (3%)
  local copies, waits for them, and re-layouts  9.33 us (2%)
    psum x1, waiting for transfers between devices, body(): weight_grad = lax.psum(partial_mix, ('node', 'win'))  274 us
    psum x1, waiting for transfers between devices, body(): lax.psum(jnp.concatenate([source_grad, target_grad], axis=1).astype(jnp.b...  113 us
    ppermute x4, starting transfers between devices, shifted(): return lax.ppermute(block, axis, route)  12 us
    ppermute x2, starting transfers between devices, padded(): lax.ppermute(head, axis, [((i + 1) % count, i) for i in range(ends)])  10.7 us
  transfers between devices with their start and end apart: 10, of which 6 were waited for; matrix products, arithmetic and copies ran while one was open for 3% of the time, Pallas kernels for 0%

commit v1 on v0

--- a/solution.py
+++ b/solution.py
@@ -190,8 +190,11 @@
         precision=highest,
         preferred_element_type=jnp.float32,
     )
-    vector_grad = lax.psum(
-        jnp.concatenate([source_grad, target_grad], axis=1).astype(jnp.bfloat16), "win"
+    vector_grad = jnp.sum(
+        lax.all_gather(
+            jnp.concatenate([source_grad, target_grad], axis=1).astype(jnp.bfloat16), "win"
+        ),
+        axis=0,
     ).astype(jnp.float32)
     return (layer_output, vector_grad, weight_grad)
 

time: 481 us -> 381 us (0.79)
  waiting for transfers between devices: 393 us -> 295 us
    psum x1 -> x0, waiting for transfers between devices: 113 us -> none  [body(): lax.psum(jnp.concatenate([source_grad, target_grad], axis=1).astype(jnp.b...]
    all_gather x0 -> x1, waiting for transfers between devices: none -> 67.6 us  [body(): lax.all_gather(jnp.concatenate([source_grad, target_grad], axis=1).astype...]
    psum x1, waiting for transfers between devices: 274 us -> 219 us  [body(): weight_grad = lax.psum(partial_mix, ('node', 'win'))]
  transfers between devices with their start and end apart: 10 -> 10, of which waited for: 6 -> 9; matrix products, arithmetic and copies ran while one was open for 3% -> 3% of each run, Pallas kernels for 0% -> 0%
where the time goes in v1:
time: 381 us
  waiting for transfers between devices  295 us (77%)
  starting transfers between devices  29.8 us (8%)
  matrix products  25 us (7%)
  between operations  16 us (4%)
  local copies, waits for them, and re-layouts  9.09 us (2%)
  other arithmetic  5.2 us (1%)
    psum x1, waiting for transfers between devices, body(): weight_grad = lax.psum(partial_mix, ('node', 'win'))  219 us
    all_gather x1, waiting for transfers between devices, body(): lax.all_gather(jnp.concatenate([source_grad, target_grad], axis=1).astype...  67.6 us
    ppermute x4, starting transfers between devices, shifted(): return lax.ppermute(block, axis, route)  12.7 us
    ppermute x2, starting transfers between devices, padded(): lax.ppermute(head, axis, [((i + 1) % count, i) for i in range(ends)])  10.7 us
  transfers between devices with their start and end apart: 10, of which 9 were waited for; matrix products, arithmetic and copies ran while one was open for 3% of the time, Pallas kernels for 0%

profile of v1, /device:TPU:1, one launch (start us, length us, event | category | flops | bytes accessed | tf_op | source)
XLA Modules:
  0.0 380.6 jit_solution(1788773708242798351)
XLA Ops:
  8.1 2.1 fusion.90
  10.2 2.1 fusion.85
  12.4 1.0 copy.64
  13.6 8.7 %collective-permute-start.1 = (bf16[512,384]{1,0:T(8,128)(2,1)S(1)}, bf16[512,384]{1,0:T(8,128)(2,1)S(1)}, u32[]{:S(2)}, u32[]{:S(2)}) collective-permute-start(bf16[512,384]{1,0:T(8,128)(2,1)S(1)} %pad_maximum_fusion.1), channel_id=1, source_target_pairs={{8,0},{16,8},{24,16},{32,24},{40,32},{48,40},{56,48},{64,56},{72,6... | collective-permute-start | bytes 1179656 | tf_op jit(solution)/shard_map/ppermute | solution.py:24
  22.4 1.9 collective-permute-start
  25.6 3.5 collective-permute-done
  29.9 4.3 %fusion.6 = (f32[512]{0:T(512)S(1)}, bf16[512,1536]{1,0:T(8,128)(2,1)S(1)}, f32[512,1536]{1,0:T(8,128)}) fusion(s32[1536]{0:T(1024)S(1)} %get-tuple-element.22, s32[512]{0:T(512)S(1)} %and_select_fusion.1, pred[1536]{0:T(1024)(128)(4,1)S(1)} %get-tuple-element.21, s32[1536]{0:T(1024)S(1)} %iota_add_fusion, s32[512]{0:T(512)S(1)} %iota_add_fusion.1, ...), kind=kOutput, calls=%fused_computation.12 | convolution fusion | flops 211025408 | bytes 5262848 | tf_op jit(solution)/shard_map/dot_general | solution.py:105
  34.2 1.5 add_convert_fusion.2
  35.7 1.9 collective-permute-start.3
  37.6 4.4 %collective-permute-start.2 = (bf16[512,256]{1,0:T(8,128)(2,1)}, bf16[512,256]{1,0:T(8,128)(2,1)}, u32[]{:S(2)}, u32[]{:S(2)}) collective-permute-start(bf16[512,256]{1,0:T(8,128)(2,1)} %get-tuple-element.36), channel_id=1, source_target_pairs={{0,8},{8,16},{16,24},{24,32},{32,40},{40,48},{48,56},{56,64},{64,7... | collective-permute-start | bytes 786440 | tf_op jit(solution)/shard_map/ppermute | solution.py:22
  42.0 1.0 convolution_multiply_fusion.1
  43.0 1.0 mul.107
  44.5 1.2 collective-permute-done.2
  45.6 3.2 multiply_reduce_fusion
  48.8 2.1 fusion.91
  51.0 0.8 fusion.88
  51.8 1.9 collective-permute-start.4
  53.7 4.4 %collective-permute-start.5 = (bf16[512,256]{1,0:T(8,128)(2,1)}, bf16[512,256]{1,0:T(8,128)(2,1)}, u32[]{:S(2)}, u32[]{:S(2)}) collective-permute-start(bf16[512,256]{1,0:T(8,128)(2,1)} %get-tuple-element.28), channel_id=1, source_target_pairs={{0,8},{8,16},{16,24},{24,32},{32,40},{40,48},{48,56},{56,64},{64,7... | collective-permute-start | bytes 786440 | tf_op jit(solution)/shard_map/ppermute | solution.py:34
  58.1 1.0 fusion.57
  59.1 0.9 reshape.141
  60.5 1.2 collective-permute-done.5
  61.7 1.6 multiply_reduce_fusion.1
  63.4 3.9 %fusion.5 = bf16[512,1536]{1,0:T(8,128)(2,1)S(1)} fusion(f32[512,1536]{1,0:T(8,128)} %get-tuple-element.35, bf16[512,256]{1,0:T(8,128)(2,1)} %collective-permute-done.3, bf16[512,256]{1,0:T(8,128)(2,1)} %get-tuple-element.36, bf16[512,256]{1,0:T(8,128)(2,1)} %collective-permute-done.2, bf16[1536,256]{1,0:T(8,128)(2,1)S(1)} %slice-done, f32[512]{0:T(512)S(1)} %add.100, ...), kind=kOutput, calls=%fused_computation.10 | convolution fusion | flops 821297152 | bytes 6827520 | tf_op jit(solution)/shard_map/dot_general | solution.py:162
  67.8 2.1 collective-permute-start.6
  69.9 4.4 %collective-permute-start.7 = (bf16[512,128]{0,1:T(8,128)(2,1)S(1)}, bf16[512,128]{0,1:T(8,128)(2,1)S(1)}, u32[]{:S(2)}, u32[]{:S(2)}) collective-permute-start(bf16[512,128]{0,1:T(8,128)(2,1)S(1)} %get-tuple-element.31), channel_id=1, source_target_pairs={{0,8},{8,16},{16,24},{24,32},{32,40},{40,48},{48,56},{56,64},{64,7... | collective-permute-start | bytes 393224 | tf_op jit(solution)/shard_map/ppermute | solution.py:34
  75.0 1.2 collective-permute-done.7
  79.0 1.0 reshape.137
  81.6 0.9 fusion.14
  82.5 67.6 %all-gather.2.cloned.1.call-done = bf16[8,512,128]{2,1,0:T(8,128)(2,1)} async-done(((bf16[1,512,128]{2,1,0:T(8,128)(2,1)}), bf16[8,512,128]{2,1,0:T(8,128)(2,1)}) %all-gather.2.cloned.1.call-update) | async-done | bytes 1048592 | tf_op jit(solution)/shard_map/all_gather | solution.py:194
  150.1 1.4 reduce_sum.62
  152.4 219.1 %all-reduce.2.cloned.1.call-done = f32[3,128,128]{2,1,0:T(8,128)} async-done(((f32[3,128,128]{2,1,0:T(8,128)}), f32[3,128,128]{2,1,0:T(8,128)}) %all-reduce.2.cloned.1.call-update) | async-done | bytes 196624 | tf_op jit(solution)/shard_map/psum | solution.py:148
  371.5 1.6 copy.66
  (92 shorter events, 9.6 us)
Async XLA Ops:
  8.0 34.0 %copy-start = (bf16[512,1,2,128]{3,2,1,0:T(2,128)(2,1)S(1)}, bf16[512,1,2,128]{3,2,1,0:T(2,128)(2,1)}, u32[]{:S(2)}) copy-start(bf16[512,1,2,128]{3,2,1,0:T(2,128)(2,1)} %param.11) | copy-start | bytes 786436
  8.0 16.3 %copy-start.24 = (s32[128]{0:T(128)S(1)}, s32[128]{0:T(128)}, u32[]{:S(2)}) copy-start(s32[128]{0:T(128)} %param.10) | copy-start | bytes 1540
  8.0 142.1 %all-gather.2.cloned.1.call-start = ((), (), s32[]{:S(2)}) async-start(), calls=%async_computation | async-start | bytes 1179648 | tf_op jit(solution)/shard_map/all_gather | solution.py:194
  10.2 15.4 %copy-start.9 = (bf16[512,64]{0,1:T(8,128)(2,1)}, bf16[512,64]{0,1:T(8,128)(2,1)S(1)}, u32[]{:S(2)}) copy-start(bf16[512,64]{0,1:T(8,128)(2,1)S(1)} %get-tuple-element.32) | copy-start | bytes 196612
  13.6 11.9 %collective-permute-start.1 = (bf16[512,384]{1,0:T(8,128)(2,1)S(1)}, bf16[512,384]{1,0:T(8,128)(2,1)S(1)}, u32[]{:S(2)}, u32[]{:S(2)}) collective-permute-start(bf16[512,384]{1,0:T(8,128)(2,1)S(1)} %pad_maximum_fusion.1), channel_id=1, source_target_pairs={{8,0},{16,8},{24,16},{32,24},{40,32},{48,40},{56,48},{64,56},{72,6... | collective-permute-start | bytes 1179656 | tf_op jit(solution)/shard_map/ppermute | solution.py:24
  22.4 6.6 %collective-permute-start = (bf16[512,384]{1,0:T(8,128)(2,1)S(1)}, bf16[512,384]{1,0:T(8,128)(2,1)S(1)}, u32[]{:S(2)}, u32[]{:S(2)}) collective-permute-start(bf16[512,384]{1,0:T(8,128)(2,1)S(1)} %pad_maximum_fusion.1), channel_id=1, source_target_pairs={{0,8},{8,16},{16,24},{24,32},{32,40},{40,48},{48,56},{56,64},{64,7... | collective-permute-start | bytes 1179656 | tf_op jit(solution)/shard_map/ppermute | solution.py:22
  25.0 9.2 %copy-start.22 = (s32[512]{0:T(512)}, s32[512]{0:T(512)S(1)}, u32[]{:S(2)}) copy-start(s32[512]{0:T(512)S(1)} %and_select_fusion.1) | copy-start | bytes 6148
  29.2 30.8 %copy-start.1 = (bf16[1536,384]{1,0:T(8,128)(2,1)}, bf16[1536,384]{1,0:T(8,128)(2,1)S(1)}, u32[]{:S(2)}) copy-start(bf16[1536,384]{1,0:T(8,128)(2,1)S(1)} %pad_maximum_fusion) | copy-start | bytes 3538948
  29.4 4.8 %copy-start.2 = (bf16[1536,64]{1,0:T(8,128)(2,1)}, bf16[1536,64]{1,0:T(8,128)(2,1)S(1)}, u32[]{:S(2)}) copy-start(bf16[1536,64]{1,0:T(8,128)(2,1)S(1)} %get-tuple-element.25) | copy-start | bytes 589828
  29.4 4.8 %copy-start.4 = (bf16[1536,64]{1,0:T(8,128)(2,1)}, bf16[1536,64]{1,0:T(8,128)(2,1)S(1)}, u32[]{:S(2)}) copy-start(bf16[1536,64]{1,0:T(8,128)(2,1)S(1)} %get-tuple-element.26) | copy-start | bytes 589828
  29.9 4.3 %copy-start.7 = (bf16[512,1,2,128]{3,2,1,0:T(2,128)(2,1)S(1)}, bf16[512,1,2,128]{3,2,1,0:T(2,128)(2,1)}, u32[]{:S(2)}) copy-start(bf16[512,1,2,128]{3,2,1,0:T(2,128)(2,1)} %param.6) | copy-start | bytes 786436
  34.2 11.4 %copy-start.6 = (bf16[512,1536]{1,0:T(8,128)(2,1)}, bf16[512,1536]{1,0:T(8,128)(2,1)S(1)}, u32[]{:S(2)}) copy-start(bf16[512,1536]{1,0:T(8,128)(2,1)S(1)} %get-tuple-element.24) | copy-start | bytes 4718596
  35.7 8.7 %collective-permute-start.3 = (bf16[512,256]{1,0:T(8,128)(2,1)}, bf16[512,256]{1,0:T(8,128)(2,1)}, u32[]{:S(2)}, u32[]{:S(2)}) collective-permute-start(bf16[512,256]{1,0:T(8,128)(2,1)} %get-tuple-element.36), channel_id=1, source_target_pairs={{8,0},{16,8},{24,16},{32,24},{40,32},{48,40},{56,48},{64,56},{72,6... | collective-permute-start | bytes 786440 | tf_op jit(solution)/shard_map/ppermute | solution.py:24
  37.6 8.0 %collective-permute-start.2 = (bf16[512,256]{1,0:T(8,128)(2,1)}, bf16[512,256]{1,0:T(8,128)(2,1)}, u32[]{:S(2)}, u32[]{:S(2)}) collective-permute-start(bf16[512,256]{1,0:T(8,128)(2,1)} %get-tuple-element.36), channel_id=1, source_target_pairs={{0,8},{8,16},{16,24},{24,32},{32,40},{40,48},{48,56},{56,64},{64,7... | collective-permute-start | bytes 786440 | tf_op jit(solution)/shard_map/ppermute | solution.py:22
  48.8 3.0 copy-start.15
  51.8 8.7 %collective-permute-start.4 = (bf16[512,256]{1,0:T(8,128)(2,1)}, bf16[512,256]{1,0:T(8,128)(2,1)}, u32[]{:S(2)}, u32[]{:S(2)}) collective-permute-start(bf16[512,256]{1,0:T(8,128)(2,1)} %get-tuple-element.27), channel_id=1, source_target_pairs={{8,0},{16,8},{24,16},{32,24},{40,32},{48,40},{56,48},{64,56},{72,6... | collective-permute-start | bytes 786440 | tf_op jit(solution)/shard_map/ppermute | solution.py:34
  53.7 8.0 %collective-permute-start.5 = (bf16[512,256]{1,0:T(8,128)(2,1)}, bf16[512,256]{1,0:T(8,128)(2,1)}, u32[]{:S(2)}, u32[]{:S(2)}) collective-permute-start(bf16[512,256]{1,0:T(8,128)(2,1)} %get-tuple-element.28), channel_id=1, source_target_pairs={{0,8},{8,16},{16,24},{24,32},{32,40},{40,48},{48,56},{56,64},{64,7... | collective-permute-start | bytes 786440 | tf_op jit(solution)/shard_map/ppermute | solution.py:34
  60.1 3.3 copy-start.21
  60.1 3.3 copy-start.16
  60.1 3.3 copy-start.23
  60.1 3.3 slice-start
  63.4 4.0 %copy-start.11 = (bf16[512,64]{0,1:T(8,128)(2,1)S(1)}, bf16[512,64]{0,1:T(8,128)(2,1)}, u32[]{:S(2)}) copy-start(bf16[512,64]{0,1:T(8,128)(2,1)} %copy-done.9) | copy-start | bytes 196612
  63.4 4.0 %copy-start.17 = (bf16[512,64]{0,1:T(8,128)(2,1)S(1)}, bf16[512,64]{0,1:T(8,128)(2,1)}, u32[]{:S(2)}) copy-start(bf16[512,64]{0,1:T(8,128)(2,1)} %get-tuple-element.15) | copy-start | bytes 196612
  67.3 8.9 %copy-start.3 = (bf16[1536,64]{1,0:T(8,128)(2,1)S(1)}, bf16[1536,64]{1,0:T(8,128)(2,1)}, u32[]{:S(2)}) copy-start(bf16[1536,64]{1,0:T(8,128)(2,1)} %copy-done.2) | copy-start | bytes 589828
  67.3 8.9 %copy-start.5 = (bf16[1536,64]{1,0:T(8,128)(2,1)S(1)}, bf16[1536,64]{1,0:T(8,128)(2,1)}, u32[]{:S(2)}) copy-start(bf16[1536,64]{1,0:T(8,128)(2,1)} %copy-done.4) | copy-start | bytes 589828
  67.7 9.3 %copy-start.13 = (f32[512,64]{0,1:T(8,128)S(1)}, f32[512,64]{0,1:T(8,128)}, u32[]{:S(2)}) copy-start(f32[512,64]{0,1:T(8,128)} %get-tuple-element.33) | copy-start | bytes 393220
  67.7 9.3 %copy-start.20 = (f32[2,64,64]{2,1,0:T(8,128)S(1)}, f32[2,64,64]{2,1,0:T(8,128)}, u32[]{:S(2)}) copy-start(f32[2,64,64]{2,1,0:T(8,128)} %param.8) | copy-start | bytes 98308
  67.8 9.6 %copy-start.12 = (f32[512,64]{0,1:T(8,128)S(1)}, f32[512,64]{0,1:T(8,128)}, u32[]{:S(2)}) copy-start(f32[512,64]{0,1:T(8,128)} %get-tuple-element.34) | copy-start | bytes 393220
  67.8 10.7 %copy-start.8 = (bf16[512,1,2,128]{3,2,1,0:T(2,128)(2,1)S(1)}, bf16[512,1,2,128]{3,2,1,0:T(2,128)(2,1)}, u32[]{:S(2)}) copy-start(bf16[512,1,2,128]{3,2,1,0:T(2,128)(2,1)} %param.6) | copy-start | bytes 786436
  67.8 7.2 %collective-permute-start.6 = (bf16[512,128]{0,1:T(8,128)(2,1)S(1)}, bf16[512,128]{0,1:T(8,128)(2,1)S(1)}, u32[]{:S(2)}, u32[]{:S(2)}) collective-permute-start(bf16[512,128]{0,1:T(8,128)(2,1)S(1)} %get-tuple-element.30), channel_id=1, source_target_pairs={{8,0},{16,8},{24,16},{32,24},{40,32},{48,40},{56,48},{64,56},{72,6... | collective-permute-start | bytes 393224 | tf_op jit(solution)/shard_map/ppermute | solution.py:34
  69.9 6.3 %collective-permute-start.7 = (bf16[512,128]{0,1:T(8,128)(2,1)S(1)}, bf16[512,128]{0,1:T(8,128)(2,1)S(1)}, u32[]{:S(2)}, u32[]{:S(2)}) collective-permute-start(bf16[512,128]{0,1:T(8,128)(2,1)S(1)} %get-tuple-element.31), channel_id=1, source_target_pairs={{0,8},{8,16},{16,24},{24,32},{32,40},{40,48},{48,56},{56,64},{64,7... | collective-permute-start | bytes 393224 | tf_op jit(solution)/shard_map/ppermute | solution.py:34
  78.4 293.1 %all-reduce.2.cloned.1.call-start = ((), (), s32[]{:S(2)}) async-start(), calls=%async_computation.1 | async-start | bytes 393216 | tf_op jit(solution)/shard_map/psum | solution.py:148
  (4 other events, 7.5 us)
Sparse Core Ops, SparseCore 0:
  78.5 71.5 all-gather.1
Sparse Core Ops, SparseCore 1:
  84.5 287.0 all-reduce.1
